TPU v7x, 32 devices: a whole 2x2x4 slice. The times are simulated.
32 devices in a mesh: row: 8 (over y, x, core), col: 4 (over z).
Axes of the slice: x: 2, y: 2, z: 4, core: 2. Of those that a mesh axis runs over, the one named last changes fastest.
Arguments:
- pair: bfloat16 [256, 256, 128], P('row', 'col'), may hold values from -6 to 6
- cotangent: bfloat16 [256, 256, 128], P('row', 'col'), may hold values from -6 to 6
- length: int32 [1], replicated, may hold values from 128 to 256
- norm_gain: float32 [128], replicated, may hold values from 0.1 to 1.9
- norm_bias: float32 [128], replicated, may hold values from -1.5 to 1.5
- left_weight: bfloat16 [128, 256], replicated, may hold values from -0.5 to 0.5
- right_weight: bfloat16 [128, 256], replicated, may hold values from -0.5 to 0.5
- gate_weight: bfloat16 [128, 128], replicated, may hold values from -0.5 to 0.5
- out_gain: float32 [128], replicated, may hold values from 0.1 to 1.9
- out_bias: float32 [128], replicated, may hold values from -2 to 2
- out_weight: bfloat16 [128, 128], replicated, may hold values from -0.5 to 0.5
Outputs:
- update: bfloat16 [256, 256, 128], P('row', 'col')
- grad_pair: bfloat16 [256, 256, 128], P('row', 'col')
- grad_left: float32 [128, 256], replicated
- grad_right: float32 [128, 256], replicated
- grad_gating: float32 [128, 128], replicated
- grad_output: float32 [128, 128], replicated
- grad_norms: float32 [4, 128], replicated
Inputs may be any that keep to these rules, and one draw needn't show every extreme that they name: Tokens at positions 255 down to length are padding.
All inputs are finite; a program needn't handle non-finite values.
Results may differ from a plain program's by a relative error of at most 0.014.
Values may be sent and summed in bfloat16 or wider, within the bound.
No kernel may reach another device: no remote copies, remote signals or barrier semaphores. Data moves between devices by JAX's collectives and lax.ppermute only.
A program may use at most 128 MiB of HBM per device.

v0:
```python
import jax
import jax.numpy as jnp
from jax import lax
from jax.sharding import PartitionSpec as P

EPS = 1e-05


def broadcast(block, axis, holder):
    block = jnp.where(lax.axis_index(axis) == holder, block, jnp.zeros_like(block))
    return lax.psum(block, axis)


def normalize(values):
    center = values - jnp.mean(values, axis=-1, keepdims=True)
    inverse = lax.rsqrt(jnp.mean(center * center, axis=-1, keepdims=True) + EPS)
    return (center * inverse, inverse)


def gating(panel, weight, first_ok, second_ok, hidden):
    projected = jnp.einsum("ikc,ch->ikh", panel, weight, preferred_element_type=jnp.float32)
    values = projected[..., :hidden]
    sigmoid_val = jax.nn.sigmoid(projected[..., hidden:])
    pad_mask = (first_ok[:, None] & second_ok[None, :]).astype(jnp.float32)[..., None]
    return ((pad_mask * sigmoid_val * values).astype(jnp.bfloat16), values, sigmoid_val, pad_mask)


def push_back(partial_value, values, sigmoid_val, pad_mask, weight, panel):
    combined = jnp.concatenate(
        [
            partial_value * pad_mask * sigmoid_val,
            partial_value * pad_mask * values * sigmoid_val * (1.0 - sigmoid_val),
        ],
        axis=-1,
    ).astype(jnp.bfloat16)
    panel_grad = jnp.einsum("ikh,ch->ikc", combined, weight, preferred_element_type=jnp.float32)
    weight_grad = jnp.einsum("ikc,ikh->ch", panel, combined, preferred_element_type=jnp.float32)
    return (panel_grad, weight_grad)


def per_device(
    pair,
    cotangent,
    length,
    norm_gain,
    norm_bias,
    left_weight,
    right_weight,
    gate_weight,
    out_gain,
    out_bias,
    out_weight,
):
    row_index = lax.axis_index("row")
    col_index = lax.axis_index("col")
    n_row = lax.axis_size("row")
    n_col = lax.axis_size("col")
    per_col = n_row // n_col
    rows_dev = pair.shape[0]
    cols_dev = pair.shape[1]
    tokens = rows_dev * n_row
    hidden = out_weight.shape[0]
    pair_hat, pair_scale = normalize(pair.astype(jnp.float32))
    normed = (pair_hat * norm_gain + norm_bias).astype(jnp.bfloat16)
    real_count = length[0]
    second_ok = jnp.arange(tokens, dtype=jnp.int32) < real_count
    own_ok = row_index * rows_dev + jnp.arange(rows_dev, dtype=jnp.int32) < real_count
    partner_ok = col_index * cols_dev + jnp.arange(cols_dev, dtype=jnp.int32) < real_count
    left_tile, left_val, left_sig, tile_mask = gating(
        normed, left_weight, own_ok, partner_ok, hidden
    )
    right_tile, right_val, right_sig, unused_mask = gating(
        normed, right_weight, own_ok, partner_ok, hidden
    )
    row_panel = lax.all_gather(normed, "col", axis=1, tiled=True)
    pieces = []
    for member in range(per_col):
        pieces.append(broadcast(row_panel, "row", col_index * per_col + member))
    col_panel = jnp.concatenate(pieces, axis=0)
    left_act = gating(row_panel, left_weight, own_ok, second_ok, hidden)[0]
    right_act = gating(col_panel, right_weight, partner_ok, second_ok, hidden)[0]
    tri = jnp.einsum("ikh,jkh->ijh", left_act, right_act, preferred_element_type=jnp.float32)
    tri_hat, tri_scale = normalize(tri)
    tri_normed = (tri_hat * out_gain + out_bias).astype(jnp.bfloat16)
    outer_val = jnp.einsum(
        "ijh,hc->ijc", tri_normed, out_weight, preferred_element_type=jnp.float32
    )
    gate_val = jax.nn.sigmoid(
        jnp.einsum("ijc,cd->ijd", normed, gate_weight, preferred_element_type=jnp.float32)
    )
    update = (gate_val * outer_val).astype(jnp.bfloat16)
    upstream = cotangent.astype(jnp.float32)
    outer_grad = (upstream * gate_val).astype(jnp.bfloat16)
    gate_grad = (upstream * outer_val * gate_val * (1.0 - gate_val)).astype(jnp.bfloat16)
    grad_output = jnp.einsum(
        "ijh,ijc->hc", tri_normed, outer_grad, preferred_element_type=jnp.float32
    )
    grad_gating = jnp.einsum("ijc,ijd->cd", normed, gate_grad, preferred_element_type=jnp.float32)
    tnorm_grad = jnp.einsum(
        "ijc,hc->ijh", outer_grad, out_weight, preferred_element_type=jnp.float32
    )
    hat_grad = tnorm_grad * out_gain
    tri_grad = (
        tri_scale
        * (
            hat_grad
            - jnp.mean(hat_grad, axis=-1, keepdims=True)
            - tri_hat * jnp.mean(hat_grad * tri_hat, axis=-1, keepdims=True)
        )
    ).astype(jnp.bfloat16)
    row_partial = jnp.einsum(
        "ijh,jkh->ikh", tri_grad, right_act, preferred_element_type=jnp.float32
    )
    col_partial = jnp.einsum("ijh,ikh->jkh", tri_grad, left_act, preferred_element_type=jnp.float32)
    row_part = lax.psum_scatter(
        row_partial.astype(jnp.bfloat16), "col", scatter_dimension=1, tiled=True
    ).astype(jnp.float32)
    summed = lax.psum_scatter(
        col_partial.astype(jnp.bfloat16), "row", scatter_dimension=0, tiled=True
    )
    slab = summed[None]
    received = lax.all_to_all(slab, "col", split_axis=2, concat_axis=0, tiled=True)
    select = (jnp.arange(per_col, dtype=jnp.int32) == row_index // n_col).astype(jnp.bfloat16)
    spread = (received[:, None] * select[None, :, None, None, None]).reshape(
        (n_row,) + received.shape[1:]
    )
    returned = lax.all_to_all(spread, "row", split_axis=0, concat_axis=0, tiled=True)
    start = row_index % per_col * n_col
    owned = lax.dynamic_slice_in_dim(returned, start, n_col, 0).reshape(rows_dev, cols_dev, -1)
    col_part = owned.astype(jnp.float32)
    from_rows, grad_left = push_back(row_part, left_val, left_sig, tile_mask, left_weight, normed)
    from_cols, grad_right = push_back(
        col_part, right_val, right_sig, tile_mask, right_weight, normed
    )
    gate_back = jnp.einsum(
        "ijd,cd->ijc", gate_grad, gate_weight, preferred_element_type=jnp.float32
    )
    normed_grad = gate_back + from_rows + from_cols
    scaled = normed_grad * norm_gain
    grad_pair = (
        pair_scale
        * (
            scaled
            - jnp.mean(scaled, axis=-1, keepdims=True)
            - pair_hat * jnp.mean(scaled * pair_hat, axis=-1, keepdims=True)
        )
    ).astype(jnp.bfloat16)
    grad_norms = jnp.stack(
        [
            jnp.sum(normed_grad * pair_hat, axis=(0, 1)),
            jnp.sum(normed_grad, axis=(0, 1)),
            jnp.sum(tnorm_grad * tri_hat, axis=(0, 1)),
            jnp.sum(tnorm_grad, axis=(0, 1)),
        ]
    )
    totals = lax.psum((grad_left, grad_right, grad_gating, grad_output, grad_norms), ("row", "col"))
    inverse = 1.0 / tokens
    return (
        update,
        grad_pair,
        totals[0] * inverse,
        totals[1] * inverse,
        totals[2] * inverse,
        totals[3] * inverse,
        totals[4] * inverse,
    )


def solution(mesh):
    return jax.shard_map(
        per_device,
        mesh=mesh,
        in_specs=(
            P("row", "col", None),
            P("row", "col", None),
            P(),
            P(),
            P(),
            P(),
            P(),
            P(),
            P(),
            P(),
            P(),
        ),
        out_specs=(P("row", "col", None), P("row", "col", None), P(), P(), P(), P(), P()),
        check_vma=False,
    )
```

profile of v0, /device:TPU:0, one launch (start us, length us, event | category | flops | bytes accessed | tf_op | source)
XLA Modules:
  0.0 473.8 jit_solution(4896643660126480447)
XLA Ops:
  10.3 2.5 fusion.25
  14.4 47.0 %all-gather.2.cloned.1.call-done = bf16[32,256,128]{2,1,0:T(8,128)(2,1)} async-done(((bf16[32,64,128]{2,1,0:T(8,128)(2,1)}), bf16[32,256,128]{2,1,0:T(8,128)(2,1)}) %all-gather.2.cloned.1.call-update) | async-done | bytes 2097168 | tf_op jit(solution)/shard_map/all_gather | solution.py:75
  61.4 3.8 broadcast_select_fusion.1
  68.3 3.1 copy.54
  71.5 2.8 fusion.53
  74.4 2.7 fusion.5
  77.0 4.6 copy.52
  81.6 63.4 %all-reduce.7.cloned.1.call-done = (bf16[32,256,128]{2,1,0:T(8,128)(2,1)}, bf16[32,256,128]{2,1,0:T(8,128)(2,1)}) async-done(((bf16[32,256,128]{2,1,0:T(8,128)(2,1)}, bf16[32,256,128]{2,1,0:T(8,128)(2,1)}), (bf16[32,256,128]{2,1,0:T(8,128)(2,1)}, bf16[32,256,128]{2,1,0:T(8,128)(2,1)})) %all-reduce.7.cloned.1.call-update) | async-done | bytes 4194320 | tf_op jit(solution)/shard_map/psum | solution.py:11
  145.1 4.5 fusion.10
  149.6 4.3 fusion
  154.0 6.8 %copy.51 = bf16[64,256,128]{1,0,2:T(8,128)(2,1)} copy(bf16[64,256,128]{2,1,0:T(8,128)(2,1)} %fusion) | data formatting | bytes 8388608 | tf_op jit(solution)/shard_map/convert_element_type | solution.py:25
  160.7 4.1 bitcast_reduce_fusion
  169.9 2.2 copy.66
  173.4 4.3 fusion.75
  177.7 4.6 copy.56
  182.5 41.1 %reduce-scatter.7.cloned.1.call-done = bf16[8,32768]{1,0:T(8,128)(2,1)} async-done(((bf16[64,32768]{1,0:T(8,128)(2,1)}), bf16[8,32768]{1,0:T(8,128)(2,1)}) %reduce-scatter.7.cloned.1.call-update) | async-done | bytes 524304
  226.4 4.6 all-to-all-start
  235.7 23.9 %all-to-all-done = bf16[1,8,256,128]{3,1,0,2:T(8,128)(2,1)} async-done(((bf16[1,8,256,128]{3,1,0,2:T(8,128)(2,1)}), bf16[1,8,256,128]{3,1,0,2:T(8,128)(2,1)}, u32[]{:S(2)}, u32[]{:S(2)}) %all-to-all-start) | async-done | bytes 524320 | tf_op jit(solution)/shard_map/all_to_all | solution.py:122
  261.9 4.2 all-to-all-start.1
  269.7 11.9 %all-to-all-done.1 = bf16[8,8,64,128]{3,2,1,0:T(8,128)(2,1)} async-done(((bf16[8,8,64,128]{3,2,1,0:T(8,128)(2,1)}), bf16[8,8,64,128]{3,2,1,0:T(8,128)(2,1)}, u32[]{:S(2)}, u32[]{:S(2)}) %all-to-all-start.1) | async-done | bytes 1048608 | tf_op jit(solution)/shard_map/all_to_all | solution.py:127
  282.7 2.8 fusion.49
  289.0 2.6 fusion.30
  291.6 37.2 %psum.55 = f32[4,128]{1,0:T(4,128)S(1)} all-reduce(f32[4,128]{1,0:T(4,128)S(1)} %pad_maximum_fusion.6), channel_id=1, replica_groups=mesh['row'=8,'col'=4] {'row','col'}, use_global_device_ids=true, to_apply=%region_20.21 | all-reduce | flops 512 | bytes 4096 | tf_op jit(solution)/shard_map/psum | solution.py:156
  331.3 129.8 %all-reduce.5.cloned.1.call-done = (f32[128,256]{1,0:T(8,128)}, f32[128,256]{1,0:T(8,128)}, f32[128,128]{1,0:T(8,128)}, f32[128,128]{1,0:T(8,128)}) async-done(((f32[128,256]{1,0:T(8,128)}, f32[128,256]{1,0:T(8,128)}, f32[128,128]{1,0:T(8,128)}, f32[128,128]{1,0:T(8,128)}), (f32[128,256]{1,0:T(8,128)}, f32[128,256]{1,0:T(8,128)}, f32[128,128]{1,0:T(8,128)}, ...) | async-done | bytes 393232 | tf_op jit(solution)/shard_map/psum | solution.py:156
  (90 shorter events, 40.0 us)
Async XLA Ops:
  7.2 137.9 %copy-start = (bf16[128,256]{1,0:T(8,128)(2,1)S(1)}, bf16[128,256]{1,0:T(8,128)(2,1)}, u32[]{:S(2)}) copy-start(bf16[128,256]{1,0:T(8,128)(2,1)} %param.17) | copy-start | bytes 196612
  7.2 5.7 %copy-start.12 = (bf16[128,128]{1,0:T(8,128)(2,1)S(1)}, bf16[128,128]{1,0:T(8,128)(2,1)}, u32[]{:S(2)}) copy-start(bf16[128,128]{1,0:T(8,128)(2,1)} %param.18) | copy-start | bytes 98308
  7.2 54.2 %all-gather.2.cloned.1.call-start = ((), (), s32[]{:S(2)}) async-start(), calls=%async_computation.4 | async-start | bytes 2621440 | tf_op jit(solution)/shard_map/all_gather | solution.py:75
  12.8 132.2 %all-reduce.7.cloned.1.call-start = ((), (), s32[]{:S(2)}) async-start(), calls=%async_computation.8 | async-start | bytes 8388608 | tf_op jit(solution)/shard_map/psum | solution.py:11
  65.2 1.0 copy-start.6
  65.2 1.0 copy-start.11
  65.2 158.4 %reduce-scatter.7.cloned.1.call-start = ((), (), s32[]{:S(2)}) async-start(), calls=%async_computation.6 | async-start | bytes 4718592
  67.6 4.0 copy-start.9
  164.8 0.7 copy-start.14
  165.5 1.3 copy-start.15
  166.8 1.8 copy-start.1
  168.6 1.3 copy-start.3
  172.2 1.2 copy-start.4
  172.2 110.4 %reduce-scatter.5.cloned.1.call-start = ((), (), s32[]{:S(2)}) async-start(), calls=%async_computation.5 | async-start | bytes 2621440 | tf_op jit(solution)/shard_map/reduce_scatter | solution.py:115
  223.6 7.5 %copy-start.2 = (bf16[32,64,128]{2,1,0:T(8,128)(2,1)S(1)}, bf16[32,64,128]{2,1,0:T(8,128)(2,1)}, u32[]{:S(2)}) copy-start(bf16[32,64,128]{2,1,0:T(8,128)(2,1)} %fusion.25) | copy-start | bytes 1572868
  226.4 33.2 %all-to-all-start = ((bf16[1,8,256,128]{3,1,0,2:T(8,128)(2,1)}), bf16[1,8,256,128]{3,1,0,2:T(8,128)(2,1)}, u32[]{:S(2)}, u32[]{:S(2)}) async-start(bf16[1,8,256,128]{3,1,0,2:T(8,128)(2,1)} %copy.58), calls=%async_computation.1 | async-start | bytes 1048576 | tf_op jit(solution)/shard_map/all_to_all | solution.py:122
  231.1 3.5 copy-start.8
  260.8 5.4 %copy-start.7 = (bf16[32,64,128]{2,1,0:T(8,128)(2,1)S(1)}, bf16[32,64,128]{2,1,0:T(8,128)(2,1)}, u32[]{:S(2)}) copy-start(bf16[32,64,128]{2,1,0:T(8,128)(2,1)} %param.12) | copy-start | bytes 1572868
  261.9 19.6 %all-to-all-start.1 = ((bf16[8,8,64,128]{3,2,1,0:T(8,128)(2,1)}), bf16[8,8,64,128]{3,2,1,0:T(8,128)(2,1)}, u32[]{:S(2)}, u32[]{:S(2)}) async-start(bf16[8,8,64,128]{3,2,1,0:T(8,128)(2,1)} %bitcast_multiply_fusion), calls=%async_computation.2 | async-start | bytes 2097152 | tf_op jit(solution)/shard_map/all_to_all | solution.py:127
  266.2 195.0 %all-reduce.5.cloned.1.call-start = ((), (), s32[]{:S(2)}) async-start(), calls=%async_computation.7 | async-start | bytes 786432 | tf_op jit(solution)/shard_map/psum | solution.py:156
  285.5 2.5 copy-start.10
  286.5 2.5 copy-start.5
  286.5 2.5 copy-start.13
Sparse Core Ops, SparseCore 0:
  13.0 48.3 all-gather.1
  65.4 79.6 all-reduce.6
  172.3 51.2 reduce-scatter.6
  225.7 51.5 reduce-scatter.4
  330.9 130.2 all-reduce.4
where the time goes:
time: 475 us; the launch traced here: 474 us
  waiting for transfers between devices  317 us (67%)
  blocking collectives  37.2 us (8%)
  matrix products  32.8 us (7%)
  other arithmetic  32.6 us (7%)
  local copies, waits for them, and re-layouts  29.7 us (6%)
  between operations  14.8 us (3%)
  starting transfers between devices  9.43 us (2%)
    psum x1, waiting for transfers between devices, per_device(): lax.psum((grad_left, grad_right, grad_gating, grad_output, grad_norms), (...  130 us
    psum x1, waiting for transfers between devices, broadcast(): return lax.psum(block, axis)  63.4 us
    all_gather x1, waiting for transfers between devices, per_device(): row_panel = lax.all_gather(normed, 'col', axis=1, tiled=True)  47 us
    unnamed x6, waiting for transfers between devices  41.2 us
    psum x1, blocking collectives, per_device(): lax.psum((grad_left, grad_right, grad_gating, grad_output, grad_norms), (...  37.2 us
    all_to_all x1, waiting for transfers between devices, per_device(): lax.all_to_all(slab, 'col', split_axis=2, concat_axis=0, tiled=True)  23.9 us
    all_to_all x1, waiting for transfers between devices, per_device(): lax.all_to_all(spread, 'row', split_axis=0, concat_axis=0, tiled=True)  11.9 us
    convert_element_type x2, local copies, waits for them, and re-layouts, gating(): (pad_mask * sigmoid_val * values).astype(jnp.bfloat16)  11.4 us
  transfers between devices with their start and end apart: 7, of which 6 were waited for; matrix products, arithmetic and copies ran while one was open for 8% of the time, Pallas kernels for 0%

commit v1 on v0

--- a/solution.py
+++ b/solution.py
@@ -8,7 +8,7 @@
 
 def broadcast(block, axis, holder):
     block = jnp.where(lax.axis_index(axis) == holder, block, jnp.zeros_like(block))
-    return lax.psum(block, axis)
+    return jnp.sum(lax.all_gather(block, axis), axis=0)
 
 
 def normalize(values):

time: 475 us -> 586 us (1.23)
  waiting for transfers between devices: 317 us -> 407 us
  other arithmetic: 32.6 us -> 53.6 us
    all_gather x0 -> x2, waiting for transfers between devices: none -> 152 us  [broadcast(): return jnp.sum(lax.all_gather(block, axis), axis=0)]
    psum x1 -> x0, waiting for transfers between devices: 63.4 us -> none  [broadcast(): return lax.psum(block, axis)]
    reduce_sum x0 -> x2, other arithmetic: none -> 21.1 us  [broadcast(): return jnp.sum(lax.all_gather(block, axis), axis=0)]
    unnamed x6 -> x7, waiting for transfers between devices: 41.2 us -> 41.8 us
  transfers between devices with their start and end apart: 7 -> 8, of which waited for: 6 -> 7; matrix products, arithmetic and copies ran while one was open for 8% -> 9% of each run, Pallas kernels for 0% -> 0%
where the time goes in v1:
time: 586 us; the launch traced here: 584 us
  waiting for transfers between devices  407 us (69%)
  other arithmetic  53.6 us (9%)
  blocking collectives  37.2 us (6%)
  matrix products  33.2 us (6%)
  local copies, waits for them, and re-layouts  29.2 us (5%)
  between operations  15.1 us (3%)
  starting transfers between devices  9.09 us (2%)
    all_gather x2, waiting for transfers between devices, broadcast(): return jnp.sum(lax.all_gather(block, axis), axis=0)  152 us
    psum x1, waiting for transfers between devices, per_device(): lax.psum((grad_left, grad_right, grad_gating, grad_output, grad_norms), (...  130 us
    all_gather x1, waiting for transfers between devices, per_device(): row_panel = lax.all_gather(normed, 'col', axis=1, tiled=True)  48.5 us
    unnamed x7, waiting for transfers between devices  41.8 us
    psum x1, blocking collectives, per_device(): lax.psum((grad_left, grad_right, grad_gating, grad_output, grad_norms), (...  37.2 us
    all_to_all x1, waiting for transfers between devices, per_device(): lax.all_to_all(slab, 'col', split_axis=2, concat_axis=0, tiled=True)  23.8 us
    reduce_sum x2, other arithmetic, broadcast(): return jnp.sum(lax.all_gather(block, axis), axis=0)  21.1 us
  transfers between devices with their start and end apart: 8, of which 7 were waited for; matrix products, arithmetic and copies ran while one was open for 9% of the time, Pallas kernels for 0%

profile of v1, /device:TPU:0, one launch (start us, length us, event | category | flops | bytes accessed | tf_op | source)
XLA Modules:
  0.0 584.5 jit_solution(9061082145251062868)
XLA Ops:
  12.9 48.5 %all-gather.6.cloned.1.call-done = bf16[32,256,128]{2,1,0:T(8,128)(2,1)} async-done(((bf16[32,64,128]{2,1,0:T(8,128)(2,1)}), bf16[32,256,128]{2,1,0:T(8,128)(2,1)}) %all-gather.6.cloned.1.call-update) | async-done | bytes 2097168 | tf_op jit(solution)/shard_map/all_gather | solution.py:75
  61.4 3.9 broadcast_select_fusion.1
  69.1 3.1 copy.54
  72.4 3.1 fusion.53
  75.5 2.9 fusion.5
  78.4 4.6 copy.52
  83.0 71.0 %all-gather.8.cloned.1.call-done = bf16[256,256,128]{2,1,0:T(8,128)(2,1)} async-done(((bf16[32,256,128]{2,1,0:T(8,128)(2,1)}), bf16[256,256,128]{2,1,0:T(8,128)(2,1)}) %all-gather.8.cloned.1.call-update) | async-done | bytes 16777232 | tf_op jit(solution)/shard_map/all_gather | solution.py:11
  154.0 10.6 %reduce_sum.134 = bf16[32,256,128]{2,1,0:T(8,128)(2,1)} reduce(bf16[8,32,256,128]{3,2,1,0:T(8,128)(2,1)} %bitcast.113, bf16[]{:T(256)} %constant.61.clone.1), dimensions={0}, to_apply=%region_2.3 | reduce | flops 7340032 | bytes 18874370 | tf_op jit(solution)/shard_map/reduce_sum | solution.py:11
  164.6 81.1 %all-gather.10.cloned.1.call-done = bf16[256,256,128]{2,1,0:T(8,128)(2,1)} async-done(((bf16[32,256,128]{2,1,0:T(8,128)(2,1)}), bf16[256,256,128]{2,1,0:T(8,128)(2,1)}) %all-gather.10.cloned.1.call-update) | async-done | bytes 16777232 | tf_op jit(solution)/shard_map/all_gather | solution.py:11
  245.7 10.5 %reduce_sum.135 = bf16[32,256,128]{2,1,0:T(8,128)(2,1)} reduce(bf16[8,32,256,128]{3,2,1,0:T(8,128)(2,1)} %bitcast.114, bf16[]{:T(256)} %constant.61.clone.1), dimensions={0}, to_apply=%region_3.4 | reduce | flops 7340032 | bytes 18874370 | tf_op jit(solution)/shard_map/reduce_sum | solution.py:11
  256.2 4.5 fusion.10
  260.7 4.3 fusion
  265.1 6.8 %copy.51 = bf16[64,256,128]{1,0,2:T(8,128)(2,1)} copy(bf16[64,256,128]{2,1,0:T(8,128)(2,1)} %fusion) | data formatting | bytes 8388608 | tf_op jit(solution)/shard_map/convert_element_type | solution.py:25
  271.9 4.1 bitcast_reduce_fusion
  284.5 4.3 fusion.75
  288.8 4.6 copy.56
  293.6 41.1 %reduce-scatter.7.cloned.1.call-done = bf16[8,32768]{1,0:T(8,128)(2,1)} async-done(((bf16[64,32768]{1,0:T(8,128)(2,1)}), bf16[8,32768]{1,0:T(8,128)(2,1)}) %reduce-scatter.7.cloned.1.call-update) | async-done | bytes 524304
  337.4 4.6 all-to-all-start
  346.7 23.8 %all-to-all-done = bf16[1,8,256,128]{3,1,0,2:T(8,128)(2,1)S(1)} async-done(((bf16[1,8,256,128]{3,1,0,2:T(8,128)(2,1)}), bf16[1,8,256,128]{3,1,0,2:T(8,128)(2,1)S(1)}, u32[]{:S(2)}, u32[]{:S(2)}) %all-to-all-start) | async-done | bytes 524320 | tf_op jit(solution)/shard_map/all_to_all | solution.py:122
  371.9 4.2 all-to-all-start.1
  380.6 10.9 %all-to-all-done.1 = bf16[8,8,64,128]{3,2,1,0:T(8,128)(2,1)} async-done(((bf16[8,8,64,128]{3,2,1,0:T(8,128)(2,1)}), bf16[8,8,64,128]{3,2,1,0:T(8,128)(2,1)}, u32[]{:S(2)}, u32[]{:S(2)}) %all-to-all-start.1) | async-done | bytes 1048608 | tf_op jit(solution)/shard_map/all_to_all | solution.py:127
  399.1 2.7 fusion.30
  401.9 37.2 %psum.39 = f32[4,128]{1,0:T(4,128)S(1)} all-reduce(f32[4,128]{1,0:T(4,128)S(1)} %pad_maximum_fusion.6), channel_id=1, replica_groups=mesh['row'=8,'col'=4] {'row','col'}, use_global_device_ids=true, to_apply=%region_20.21 | all-reduce | flops 512 | bytes 4096 | tf_op jit(solution)/shard_map/psum | solution.py:156
  441.6 129.9 %all-reduce.3.cloned.1.call-done = (f32[128,256]{1,0:T(8,128)}, f32[128,256]{1,0:T(8,128)}, f32[128,128]{1,0:T(8,128)}, f32[128,128]{1,0:T(8,128)}) async-done(((f32[128,256]{1,0:T(8,128)}, f32[128,256]{1,0:T(8,128)}, f32[128,128]{1,0:T(8,128)}, f32[128,128]{1,0:T(8,128)}), (f32[128,256]{1,0:T(8,128)}, f32[128,256]{1,0:T(8,128)}, f32[128,128]{1,0:T(8,128)}, ...) | async-done | bytes 393232 | tf_op jit(solution)/shard_map/psum | solution.py:156
  (103 shorter events, 47.1 us)
Async XLA Ops:
  7.2 249.0 %copy-start = (bf16[128,256]{1,0:T(8,128)(2,1)S(1)}, bf16[128,256]{1,0:T(8,128)(2,1)}, u32[]{:S(2)}) copy-start(bf16[128,256]{1,0:T(8,128)(2,1)} %param.17) | copy-start | bytes 196612
  7.2 54.2 %all-gather.6.cloned.1.call-start = ((), (), s32[]{:S(2)}) async-start(), calls=%async_computation.4 | async-start | bytes 2621440 | tf_op jit(solution)/shard_map/all_gather | solution.py:75
  12.8 141.2 %all-gather.8.cloned.1.call-start = ((), (), s32[]{:S(2)}) async-start(), calls=%async_computation.6 | async-start | bytes 18874368 | tf_op jit(solution)/shard_map/all_gather | solution.py:11
  65.2 1.5 copy-start.2
  65.2 1.5 copy-start.16
  65.2 180.4 %all-gather.10.cloned.1.call-start = ((), (), s32[]{:S(2)}) async-start(), calls=%async_computation.7 | async-start | bytes 18874368 | tf_op jit(solution)/shard_map/all_gather | solution.py:11
  66.0 268.7 %reduce-scatter.7.cloned.1.call-start = ((), (), s32[]{:S(2)}) async-start(), calls=%async_computation.8 | async-start | bytes 4718592
  67.7 1.3 copy-start.3
  69.1 3.3 copy-start.12
  276.6 1.3 copy-start.19
  277.9 1.8 copy-start.1
  279.7 1.3 copy-start.5
  283.3 109.3 %reduce-scatter.5.cloned.1.call-start = ((), (), s32[]{:S(2)}) async-start(), calls=%async_computation.5 | async-start | bytes 2621440 | tf_op jit(solution)/shard_map/reduce_scatter | solution.py:115
  337.4 33.1 %all-to-all-start = ((bf16[1,8,256,128]{3,1,0,2:T(8,128)(2,1)}), bf16[1,8,256,128]{3,1,0,2:T(8,128)(2,1)S(1)}, u32[]{:S(2)}, u32[]{:S(2)}) async-start(bf16[1,8,256,128]{3,1,0,2:T(8,128)(2,1)} %copy.58), calls=%async_computation.1 | async-start | bytes 1048576 | tf_op jit(solution)/shard_map/all_to_all | solution.py:122
  342.1 3.5 copy-start.11
  370.6 5.5 copy-start.4
  371.9 19.6 %all-to-all-start.1 = ((bf16[8,8,64,128]{3,2,1,0:T(8,128)(2,1)}), bf16[8,8,64,128]{3,2,1,0:T(8,128)(2,1)}, u32[]{:S(2)}, u32[]{:S(2)}) async-start(bf16[8,8,64,128]{3,2,1,0:T(8,128)(2,1)} %bitcast_multiply_fusion), calls=%async_computation.2 | async-start | bytes 2097152 | tf_op jit(solution)/shard_map/all_to_all | solution.py:127
  376.1 195.4 %all-reduce.3.cloned.1.call-start = ((), (), s32[]{:S(2)}) async-start(), calls=%async_computation.9 | async-start | bytes 786432 | tf_op jit(solution)/shard_map/psum | solution.py:156
  379.3 13.3 %copy-start.7 = (f32[32,64,256]{2,1,0:T(8,128)S(1)}, f32[32,64,256]{2,1,0:T(8,128)}, u32[]{:S(2)}) copy-start(f32[32,64,256]{2,1,0:T(8,128)} %fusion.51) | copy-start | bytes 6291460
  395.0 3.1 copy-start.13
  395.0 3.1 copy-start.14
  395.0 1.6 copy-start.10
  396.7 2.5 copy-start.8
  396.7 2.5 copy-start.17
  (4 other events, 4.0 us)
Sparse Core Ops, SparseCore 0:
  12.9 48.3 all-gather.5
  65.4 88.5 all-gather.7
  155.9 89.7 all-gather.9
  283.5 51.1 reduce-scatter.6
  336.8 51.5 reduce-scatter.4
  441.2 130.3 all-reduce.2
